TPU v7x, 32 devices: a whole 2x2x4 slice. The times are simulated.
32 devices in a mesh: row: 8 (over z, y), col: 4 (over x, core).
Axes of the slice: x: 2, y: 2, z: 4, core: 2. Of those that a mesh axis runs over, the one named last changes fastest.
Arguments:
- leaf_inverse: bfloat16 [32, 1024, 1024], P(('row', 'col')), as said below
- leaf_rhs: bfloat16 [32, 1024, 512], P(('row', 'col')), may hold values from -6 to 6
- leaf_tiles: bfloat16 [32, 1024, 1024], P(('row', 'col')), may hold values from -0.09375 to 0.09375
- mid_inverse_t: bfloat16 [8, 1024, 1024], P('col', None, 'row'), as said below
- mid_rhs: bfloat16 [8, 1024, 512], P('col', 'row'), may hold values from -6 to 6
- mid_tiles: bfloat16 [8, 1024, 1024], P('col', None, 'row'), may hold values from -0.125 to 0.125
- top_inverse_t: bfloat16 [2, 1024, 1024], P(None, None, 'col'), as said below
- top_rhs: bfloat16 [2, 1024, 512], P(None, 'col'), may hold values from -6 to 6
- tile_lists: int32 [32, 1], P(('row', 'col')), may hold values from 0 to 1
Outputs:
- leaf_solved: bfloat16 [32, 1024, 512], P(('row', 'col'))
- mid_solved: bfloat16 [8, 1024, 512], P('col', 'row')
- top_solved: bfloat16 [2, 1024, 512], P(None, 'col')
Inputs may be any that keep to these rules, and one draw needn't show every extreme that they name: Each leaf_inverse[d] is zero above its diagonal and has diagonal entries between 0.75 and 1.25. Each mid_inverse_t[q] is zero below its diagonal and has diagonal entries between 0.75 and 1.25. Each top_inverse_t[b] is zero below its diagonal and has diagonal entries between 0.75 and 1.25.
All inputs are finite; a program needn't handle non-finite values.
Results may differ from a plain program's by a relative error of at most 0.0065.
Values may be sent and summed in bfloat16 or wider, within the bound.
No kernel may reach another device: no remote copies, remote signals or barrier semaphores. Data moves between devices by JAX's collectives and lax.ppermute only.
A program may use at most 64 MiB of HBM per device.

v0:
```python
import jax
import jax.numpy as jnp
from jax import lax
from jax.sharding import PartitionSpec as P

NB = 2


def solve_piece(inverse_cols, piece):
    return lax.dot_general(
        inverse_cols, piece, (((1,), (1,)), ((0,), (0,))), preferred_element_type=jnp.float32
    )


def local(
    leaf_inverse,
    leaf_rhs,
    leaf_tiles,
    mid_inverse_t,
    mid_rhs,
    mid_tiles,
    top_inverse_t,
    top_rhs,
    tile_lists,
):
    slot_ids = jnp.arange(NB, dtype=jnp.int32)[:, None, None]
    solved_leaf = jnp.dot(leaf_inverse[0], leaf_rhs[0], preferred_element_type=jnp.float32).astype(
        jnp.bfloat16
    )
    leaf_update = jnp.dot(leaf_tiles[0], solved_leaf, preferred_element_type=jnp.float32)
    mid_terms = jnp.where(slot_ids == tile_lists[0, 0], leaf_update[None], 0.0)
    mid_share = lax.psum_scatter(mid_terms, "row", scatter_dimension=1, tiled=True)
    mid_resid = (mid_rhs.astype(jnp.float32) - mid_share).astype(jnp.bfloat16)
    mid_own = solve_piece(
        mid_inverse_t, lax.all_gather(mid_resid, "row", axis=1, tiled=True)
    ).astype(jnp.bfloat16)
    top_terms = lax.dot_general(
        mid_tiles, mid_own, (((2,), (1,)), ((0,), (0,))), preferred_element_type=jnp.float32
    )
    summed_rows = lax.psum(top_terms, "row")
    top_share = lax.psum_scatter(summed_rows, "col", scatter_dimension=1, tiled=True)
    top_resid = (top_rhs.astype(jnp.float32) - top_share).astype(jnp.bfloat16)
    top_own = solve_piece(
        top_inverse_t, lax.all_gather(top_resid, "col", axis=1, tiled=True)
    ).astype(jnp.bfloat16)
    return (solved_leaf[None], mid_own, top_own)


def solution(mesh):
    placed = (
        P(("row", "col"), None, None),
        P(("row", "col"), None, None),
        P(("row", "col"), None, None),
        P("col", None, "row"),
        P("col", "row", None),
        P("col", None, "row"),
        P(None, None, "col"),
        P(None, "col", None),
        P(("row", "col"), None),
    )
    return jax.shard_map(
        local,
        mesh=mesh,
        in_specs=placed,
        out_specs=(P(("row", "col"), None, None), P("col", "row", None), P(None, "col", None)),
        check_vma=False,
    )
```

profile of v0, /device:TPU:0, one launch (start us, length us, event | category | flops | bytes accessed | tf_op | source)
XLA Modules:
  0.0 324.7 jit_solution(155862839401762226)
XLA Ops:
  7.2 0.0 copy-start
  7.2 0.0 reduce-scatter.3.cloned.1.call-start
  8.0 0.8 copy-done
  8.8 2.6 fusion.7
  11.4 0.0 copy-start.5
  11.4 1.0 copy-done.5
  12.4 1.3 fusion.4
  13.7 2.5 broadcast_select_fusion
  16.2 0.0 reduce-scatter.3.cloned.1.call-update
  16.2 0.0 all-gather.3.cloned.1.call-start
  16.3 0.9 copy-done.3
  17.2 0.2 copy.12
  17.4 90.4 %reduce-scatter.3.cloned.1.call-done = f32[2,128,512]{1,2,0:T(8,128)} async-done(((f32[2,1024,512]{1,2,0:T(8,128)}), f32[2,128,512]{1,2,0:T(8,128)}) %reduce-scatter.3.cloned.1.call-update) | async-done | bytes 524304 | tf_op jit(solution)/shard_map/reduce_scatter | solution.py:32
  107.8 1.8 subtract_convert_fusion.1
  109.6 0.0 all-gather.3.cloned.1.call-update
  109.6 0.0 reduce-scatter.5.cloned.1.call-start
  109.7 50.8 %all-gather.3.cloned.1.call-done = bf16[2,1024,512]{1,2,0:T(8,128)(2,1)} async-done(((bf16[2,128,512]{1,2,0:T(8,128)(2,1)}), bf16[2,1024,512]{1,2,0:T(8,128)(2,1)}) %all-gather.3.cloned.1.call-update) | async-done | bytes 2097168 | tf_op jit(solution)/shard_map/all_gather | solution.py:35
  160.4 2.4 convolution_convert_fusion.1
  162.8 2.7 convolution_bitcast_fusion
  165.5 0.0 reduce-scatter.5.cloned.1.call-update
  165.5 0.0 all-reduce.2.cloned.1.call-start
  165.5 42.7 %reduce-scatter.5.cloned.1.call-done = f32[2,256,512]{1,2,0:T(8,128)} async-done(((f32[2,1024,512]{1,2,0:T(8,128)}), f32[2,256,512]{1,2,0:T(8,128)}) %reduce-scatter.5.cloned.1.call-update) | async-done | bytes 1048592 | tf_op jit(solution)/shard_map/reduce_scatter | solution.py:41
  208.2 0.0 all-reduce.2.cloned.1.call-update
  208.3 0.0 all-gather.5.cloned.1.call-start
  208.3 0.2 copy.13
  208.5 81.3 %all-reduce.2.cloned.1.call-done = f32[2,256,512]{1,2,0:T(8,128)} async-done(((f32[2,256,512]{1,2,0:T(8,128)}), f32[2,256,512]{1,2,0:T(8,128)}) %all-reduce.2.cloned.1.call-update) | async-done | bytes 1048592 | tf_op jit(solution)/shard_map/psum | solution.py:40
  289.8 2.1 subtract_convert_fusion
  292.0 0.0 all-gather.5.cloned.1.call-update
  292.0 0.9 copy.14
  292.8 21.7 %all-gather.5.cloned.1.call-done = bf16[2,1024,512]{1,2,0:T(8,128)(2,1)} async-done(((bf16[2,256,512]{1,2,0:T(8,128)(2,1)}), bf16[2,1024,512]{1,2,0:T(8,128)(2,1)}) %all-gather.5.cloned.1.call-update) | async-done | bytes 2097168 | tf_op jit(solution)/shard_map/all_gather | solution.py:44
  314.6 2.6 fusion.10
  317.1 1.0 copy.15
  (8 shorter events, 0.0 us)
Async XLA Ops:
  7.2 1.6 copy-start
  7.2 100.6 %reduce-scatter.3.cloned.1.call-start = ((), (), s32[]{:S(2)}) async-start(), calls=%async_computation.2 | async-start | bytes 4718592 | tf_op jit(solution)/shard_map/reduce_scatter | solution.py:32
  8.8 3.6 %copy-start.4 = (bf16[1,1024,1024]{2,1,0:T(8,128)(2,1)S(1)}, bf16[1,1024,1024]{2,1,0:T(8,128)(2,1)}, u32[]{:S(2)}) copy-start(bf16[1,1024,1024]{2,1,0:T(8,128)(2,1)} %param.11) | copy-start | bytes 6291460
  11.4 1.0 copy-start.5
  16.2 0.9 copy-start.3
  16.2 144.2 %all-gather.3.cloned.1.call-start = ((), (), s32[]{:S(2)}) async-start(), calls=%async_computation.3 | async-start | bytes 2359296 | tf_op jit(solution)/shard_map/all_gather | solution.py:35
  17.3 145.5 %copy-start.1 = (bf16[2,1024,128]{2,1,0:T(8,128)(2,1)S(1)}, bf16[2,1024,128]{2,1,0:T(8,128)(2,1)}, u32[]{:S(2)}) copy-start(bf16[2,1024,128]{2,1,0:T(8,128)(2,1)} %param.14) | copy-start | bytes 1572868
  109.6 98.6 %reduce-scatter.5.cloned.1.call-start = ((), (), s32[]{:S(2)}) async-start(), calls=%async_computation.5 | async-start | bytes 5242880 | tf_op jit(solution)/shard_map/reduce_scatter | solution.py:41
  165.5 42.8 %copy-start.2 = (bf16[2,256,512]{2,1,0:T(8,128)(2,1)S(1)}, bf16[2,256,512]{2,1,0:T(8,128)(2,1)}, u32[]{:S(2)}) copy-start(bf16[2,256,512]{2,1,0:T(8,128)(2,1)} %param.16) | copy-start | bytes 1572868
  165.5 124.3 %all-reduce.2.cloned.1.call-start = ((), (), s32[]{:S(2)}) async-start(), calls=%async_computation.6 | async-start | bytes 2097152 | tf_op jit(solution)/shard_map/psum | solution.py:40
  208.3 106.3 %all-gather.5.cloned.1.call-start = ((), (), s32[]{:S(2)}) async-start(), calls=%async_computation.4 | async-start | bytes 2621440 | tf_op jit(solution)/shard_map/all_gather | solution.py:44
Sparse Core Ops, SparseCore 0:
  16.4 91.3 reduce-scatter.2
  110.4 49.9 all-gather.2
  165.6 42.5 reduce-scatter.4
  211.6 78.1 all-reduce.1
  292.1 22.3 all-gather.4
where the time goes:
time: 325 us
  waiting for transfers between devices  287 us (88%)
  between operations  14.6 us (4%)
  matrix products  11.5 us (4%)
  other arithmetic  6.48 us (2%)
  local copies, waits for them, and re-layouts  4.84 us (1%)
    reduce_scatter x1, waiting for transfers between devices, local(): lax.psum_scatter(mid_terms, 'row', scatter_dimension=1, tiled=True)  90.4 us
    psum x1, waiting for transfers between devices, local(): summed_rows = lax.psum(top_terms, 'row')  81.3 us
    all_gather x1, waiting for transfers between devices, local(): lax.all_gather(mid_resid, 'row', axis=1, tiled=True)  50.8 us
    reduce_scatter x1, waiting for transfers between devices, local(): lax.psum_scatter(summed_rows, 'col', scatter_dimension=1, tiled=True)  42.7 us
    all_gather x1, waiting for transfers between devices, local(): lax.all_gather(top_resid, 'col', axis=1, tiled=True)  21.7 us
  transfers between devices with their start and end apart: 5, of which 5 were waited for; matrix products, arithmetic and copies ran while one was open for 0% of the time, Pallas kernels for 0%

commit v1 on v0

--- a/solution.py
+++ b/solution.py
@@ -1,9 +1,17 @@
+import functools
 import jax
 import jax.numpy as jnp
 from jax import lax
 from jax.sharding import PartitionSpec as P
 
 NB = 2
+
+
+def _move_rings(field, dim_no):
+    return jnp.concatenate(lax.all_gather(field, "col"), dim_no)
+
+
+feed_row = functools.partial(_move_rings, dim_no=1)
 
 
 def solve_piece(inverse_cols, piece):
@@ -40,9 +48,7 @@
     summed_rows = lax.psum(top_terms, "row")
     top_share = lax.psum_scatter(summed_rows, "col", scatter_dimension=1, tiled=True)
     top_resid = (top_rhs.astype(jnp.float32) - top_share).astype(jnp.bfloat16)
-    top_own = solve_piece(
-        top_inverse_t, lax.all_gather(top_resid, "col", axis=1, tiled=True)
-    ).astype(jnp.bfloat16)
+    top_own = solve_piece(top_inverse_t, feed_row(top_resid)).astype(jnp.bfloat16)
     return (solved_leaf[None], mid_own, top_own)
 
 

time: 325 us -> 334 us (1.028)
  local copies, waits for them, and re-layouts: 4.84 us -> 14.6 us
    reshape x0 -> x1, local copies, waits for them, and re-layouts: none -> 4.43 us  [_move_rings(): return jnp.concatenate(lax.all_gather(field, 'col'), dim_no)]
    all_gather x0 -> x1, local copies, waits for them, and re-layouts: none -> 4.28 us  [_move_rings(): return jnp.concatenate(lax.all_gather(field, 'col'), dim_no)]
where the time goes in v1:
time: 334 us; the launch traced here: 333 us
  waiting for transfers between devices  287 us (86%)
  local copies, waits for them, and re-layouts  14.6 us (4%)
  between operations  14.6 us (4%)
  matrix products  11.4 us (3%)
  other arithmetic  5.68 us (2%)
    reduce_scatter x1, waiting for transfers between devices, local(): lax.psum_scatter(mid_terms, 'row', scatter_dimension=1, tiled=True)  90.4 us
    psum x1, waiting for transfers between devices, local(): summed_rows = lax.psum(top_terms, 'row')  81.4 us
    all_gather x1, waiting for transfers between devices, local(): lax.all_gather(mid_resid, 'row', axis=1, tiled=True)  50.8 us
    reduce_scatter x1, waiting for transfers between devices, local(): lax.psum_scatter(summed_rows, 'col', scatter_dimension=1, tiled=True)  42.7 us
    all_gather x1, waiting for transfers between devices, _move_rings(): return jnp.concatenate(lax.all_gather(field, 'col'), dim_no)  21.5 us
  transfers between devices with their start and end apart: 5, of which 5 were waited for; matrix products, arithmetic and copies ran while one was open for 0% of the time, Pallas kernels for 0%

profile of v1, /device:TPU:0, one launch (start us, length us, event | category | flops | bytes accessed | tf_op | source)
XLA Modules:
  0.0 333.3 jit_solution(2649638979142680234)
XLA Ops:
  7.2 0.0 reduce-scatter.3.cloned.1.call-start
  8.0 0.8 copy-done
  8.8 2.6 fusion.7
  11.4 1.0 copy-done.6
  12.4 1.3 fusion.4
  13.7 2.5 broadcast_select_fusion
  16.2 0.0 reduce-scatter.3.cloned.1.call-update
  16.2 0.0 all-gather.4.cloned.1.call-start
  16.3 0.9 copy-done.3
  17.2 0.2 copy.17
  17.4 90.4 %reduce-scatter.3.cloned.1.call-done = f32[2,128,512]{1,2,0:T(8,128)} async-done(((f32[2,1024,512]{1,2,0:T(8,128)}), f32[2,128,512]{1,2,0:T(8,128)}) %reduce-scatter.3.cloned.1.call-update) | async-done | bytes 524304 | tf_op jit(solution)/shard_map/reduce_scatter | solution.py:40
  107.8 1.8 subtract_convert_fusion.1
  109.6 0.0 all-gather.4.cloned.1.call-update
  109.6 0.0 reduce-scatter.5.cloned.1.call-start
  109.7 50.8 %all-gather.4.cloned.1.call-done = bf16[2,1024,512]{1,2,0:T(8,128)(2,1)} async-done(((bf16[2,128,512]{1,2,0:T(8,128)(2,1)}), bf16[2,1024,512]{1,2,0:T(8,128)(2,1)}) %all-gather.4.cloned.1.call-update) | async-done | bytes 2097168 | tf_op jit(solution)/shard_map/all_gather | solution.py:43
  160.4 2.3 convolution_convert_fusion.1
  162.7 2.7 convolution_bitcast_fusion
  165.4 0.0 reduce-scatter.5.cloned.1.call-update
  165.4 0.0 all-reduce.2.cloned.1.call-start
  165.5 42.7 %reduce-scatter.5.cloned.1.call-done = f32[2,256,512]{1,2,0:T(8,128)} async-done(((f32[2,1024,512]{1,2,0:T(8,128)}), f32[2,256,512]{1,2,0:T(8,128)}) %reduce-scatter.5.cloned.1.call-update) | async-done | bytes 1048592 | tf_op jit(solution)/shard_map/reduce_scatter | solution.py:49
  208.2 0.0 all-reduce.2.cloned.1.call-update
  208.2 0.0 all-gather.6.cloned.1.call-start
  208.2 0.2 copy.18
  208.4 81.4 %all-reduce.2.cloned.1.call-done = f32[2,256,512]{1,2,0:T(8,128)} async-done(((f32[2,256,512]{1,2,0:T(8,128)}), f32[2,256,512]{1,2,0:T(8,128)}) %all-reduce.2.cloned.1.call-update) | async-done | bytes 1048592 | tf_op jit(solution)/shard_map/psum | solution.py:48
  289.8 1.3 subtract_convert_fusion
  291.2 1.0 copy.19
  292.2 0.9 copy.21
  293.0 21.5 %all-gather.6.cloned.1.call-done = bf16[8,256,512]{2,1,0:T(8,128)(2,1)} async-done(((bf16[2,256,512]{2,1,0:T(8,128)(2,1)}), bf16[8,256,512]{2,1,0:T(8,128)(2,1)}) %all-gather.6.cloned.1.call-update) | async-done | bytes 2097168 | tf_op jit(solution)/shard_map/all_gather | solution.py:11
  314.5 4.3 %copy.20 = bf16[4,2,256,512]{2,0,3,1:T(4,128)(2,1)} copy(bf16[4,2,256,512]{3,2,1,0:T(8,128)(2,1)} %bitcast.35) | data formatting | bytes 4194304 | tf_op jit(solution)/shard_map/all_gather | solution.py:11
  318.8 4.4 %reshape.19 = bf16[2,1024,512]{1,2,0:T(8,128)(2,1)} reshape(bf16[2,4,256,512]{2,1,3,0:T(4,128)(2,1)} %bitcast.34) | data formatting | bytes 4194304 | tf_op jit(solution)/shard_map/reshape | solution.py:11
  323.2 2.6 fusion.10
  325.8 1.0 copy.22
  (13 shorter events, 0.1 us)
Async XLA Ops:
  7.2 1.6 copy-start
  7.2 100.6 %reduce-scatter.3.cloned.1.call-start = ((), (), s32[]{:S(2)}) async-start(), calls=%async_computation.2 | async-start | bytes 4718592 | tf_op jit(solution)/shard_map/reduce_scatter | solution.py:40
  8.8 3.6 %copy-start.4 = (bf16[1,1024,1024]{2,1,0:T(8,128)(2,1)S(1)}, bf16[1,1024,1024]{2,1,0:T(8,128)(2,1)}, u32[]{:S(2)}) copy-start(bf16[1,1024,1024]{2,1,0:T(8,128)(2,1)} %param.11) | copy-start | bytes 6291460
  11.4 1.0 copy-start.6
  16.2 0.9 copy-start.3
  16.2 144.2 %copy-start.5 = (bf16[2,1024,128]{2,1,0:T(8,128)(2,1)S(1)}, bf16[2,1024,128]{2,1,0:T(8,128)(2,1)}, u32[]{:S(2)}) copy-start(bf16[2,1024,128]{2,1,0:T(8,128)(2,1)} %param.12) | copy-start | bytes 1572868
  16.2 144.2 %all-gather.4.cloned.1.call-start = ((), (), s32[]{:S(2)}) async-start(), calls=%async_computation.3 | async-start | bytes 2359296 | tf_op jit(solution)/shard_map/all_gather | solution.py:43
  17.3 145.4 %copy-start.1 = (bf16[2,1024,128]{2,1,0:T(8,128)(2,1)S(1)}, bf16[2,1024,128]{2,1,0:T(8,128)(2,1)}, u32[]{:S(2)}) copy-start(bf16[2,1024,128]{2,1,0:T(8,128)(2,1)} %param.14) | copy-start | bytes 1572868
  109.6 98.5 %reduce-scatter.5.cloned.1.call-start = ((), (), s32[]{:S(2)}) async-start(), calls=%async_computation.5 | async-start | bytes 5242880 | tf_op jit(solution)/shard_map/reduce_scatter | solution.py:49
  165.4 42.8 %copy-start.2 = (bf16[2,256,512]{2,1,0:T(8,128)(2,1)S(1)}, bf16[2,256,512]{2,1,0:T(8,128)(2,1)}, u32[]{:S(2)}) copy-start(bf16[2,256,512]{2,1,0:T(8,128)(2,1)} %param.16) | copy-start | bytes 1572868
  165.4 124.4 %all-reduce.2.cloned.1.call-start = ((), (), s32[]{:S(2)}) async-start(), calls=%async_computation.6 | async-start | bytes 2097152 | tf_op jit(solution)/shard_map/psum | solution.py:48
  208.2 106.3 %all-gather.6.cloned.1.call-start = ((), (), s32[]{:S(2)}) async-start(), calls=%async_computation.4 | async-start | bytes 2621440 | tf_op jit(solution)/shard_map/all_gather | solution.py:11
Sparse Core Ops, SparseCore 0:
  16.4 91.3 reduce-scatter.2
  110.4 49.9 all-gather.3
  165.5 42.5 reduce-scatter.4
  211.5 78.2 all-reduce.1
  292.3 22.1 all-gather.5

commit v2 on v0

--- a/solution.py
+++ b/solution.py
@@ -1,9 +1,25 @@
+import functools
 import jax
 import jax.numpy as jnp
 from jax import lax
 from jax.sharding import PartitionSpec as P
 
 NB = 2
+
+
+def wait_area(block_here, a_name):
+    world = lax.axis_size(a_name)
+    t_next, heard = (block_here, 0)
+    while 1 << heard < world:
+        lower = lax.ppermute(
+            t_next, axis_name=a_name, perm=tuple(((no, no ^ 1 << heard) for no in range(world)))
+        )
+        t_next = t_next + lower
+        heard = heard + 1
+    return t_next
+
+
+change_the_things = functools.partial(wait_area, a_name="row")
 
 
 def solve_piece(inverse_cols, piece):
@@ -37,7 +53,7 @@
     top_terms = lax.dot_general(
         mid_tiles, mid_own, (((2,), (1,)), ((0,), (0,))), preferred_element_type=jnp.float32
     )
-    summed_rows = lax.psum(top_terms, "row")
+    summed_rows = change_the_things(top_terms)
     top_share = lax.psum_scatter(summed_rows, "col", scatter_dimension=1, tiled=True)
     top_resid = (top_rhs.astype(jnp.float32) - top_share).astype(jnp.bfloat16)
     top_own = solve_piece(

time: 325 us -> 613 us (1.89)
  waiting for transfers between devices: 287 us -> 568 us
    ppermute x0 -> x3, waiting for transfers between devices: none -> 362 us  [wait_area(): lax.ppermute(t_next, axis_name=a_name, perm=tuple(((no, no ^ 1 << heard)...]
    psum x1 -> x0, waiting for transfers between devices: 81.3 us -> none  [local(): summed_rows = lax.psum(top_terms, 'row')]
  transfers between devices with their start and end apart: 5 -> 7, of which waited for: 5 -> 7; matrix products, arithmetic and copies ran while one was open for 0% -> 0% of each run, Pallas kernels for 0% -> 0%
where the time goes in v2:
time: 613 us
  waiting for transfers between devices  568 us (93%)
  between operations  14.7 us (2%)
  other arithmetic  12.1 us (2%)
  matrix products  9.55 us (2%)
    ppermute x3, waiting for transfers between devices, wait_area(): lax.ppermute(t_next, axis_name=a_name, perm=tuple(((no, no ^ 1 << heard)...  362 us
    reduce_scatter x1, waiting for transfers between devices, local(): lax.psum_scatter(mid_terms, 'row', scatter_dimension=1, tiled=True)  90.4 us
    all_gather x1, waiting for transfers between devices, local(): lax.all_gather(mid_resid, 'row', axis=1, tiled=True)  50.8 us
    reduce_scatter x1, waiting for transfers between devices, local(): lax.psum_scatter(summed_rows, 'col', scatter_dimension=1, tiled=True)  42.3 us
    all_gather x1, waiting for transfers between devices, local(): lax.all_gather(top_resid, 'col', axis=1, tiled=True)  22.1 us
  transfers between devices with their start and end apart: 7, of which 7 were waited for; matrix products, arithmetic and copies ran while one was open for 0% of the time, Pallas kernels for 0%

profile of v2, /device:TPU:0, one launch (start us, length us, event | category | flops | bytes accessed | tf_op | source)
XLA Modules:
  0.0 612.7 jit_solution(5992569962994428248)
XLA Ops:
  8.0 0.8 copy-done
  8.8 2.6 fusion.7
  11.4 1.0 copy-done.5
  12.4 1.3 fusion.4
  13.7 2.5 broadcast_select_fusion
  16.3 0.0 all-gather.3.cloned.1.call-start
  16.3 0.9 copy-done.3
  17.2 0.2 copy.12
  17.4 90.4 %reduce-scatter.3.cloned.1.call-done = f32[2,128,512]{1,2,0:T(8,128)} async-done(((f32[2,1024,512]{1,2,0:T(8,128)}), f32[2,128,512]{1,2,0:T(8,128)}) %reduce-scatter.3.cloned.1.call-update) | async-done | bytes 524304 | tf_op jit(solution)/shard_map/reduce_scatter | solution.py:48
  107.8 1.8 subtract_convert_fusion.1
  109.6 0.0 reduce-scatter.5.cloned.1.call-start
  109.7 50.8 %all-gather.3.cloned.1.call-done = bf16[2,1024,512]{1,2,0:T(8,128)(2,1)} async-done(((bf16[2,128,512]{1,2,0:T(8,128)(2,1)}), bf16[2,1024,512]{1,2,0:T(8,128)(2,1)}) %all-gather.3.cloned.1.call-update) | async-done | bytes 2097168 | tf_op jit(solution)/shard_map/all_gather | solution.py:51
  160.4 2.4 convolution_convert_fusion.1
  162.8 0.7 convolution_bitcast_fusion
  163.5 1.5 collective-permute-start
  165.0 90.7 %collective-permute-done = f32[2,1024,512]{1,2,0:T(8,128)S(1)} collective-permute-done((f32[2,1024,512]{1,2,0:T(8,128)S(1)}, f32[2,1024,512]{1,2,0:T(8,128)S(1)}, u32[]{:S(2)}, u32[]{:S(2)}) %collective-permute-start) | collective-permute-done | bytes 4194336 | tf_op jit(solution)/shard_map/ppermute | solution.py:14
  255.7 1.4 add.13
  257.1 0.1 collective-permute-start.1
  257.2 91.3 %collective-permute-done.1 = f32[2,1024,512]{1,2,0:T(8,128)S(1)} collective-permute-done((f32[2,1024,512]{1,2,0:T(8,128)S(1)}, f32[2,1024,512]{1,2,0:T(8,128)S(1)}, u32[]{:S(2)}, u32[]{:S(2)}) %collective-permute-start.1) | collective-permute-done | bytes 4194336 | tf_op jit(solution)/shard_map/ppermute | solution.py:14
  348.4 1.4 add.14
  349.8 0.8 collective-permute-start.2
  350.6 180.5 %collective-permute-done.2 = f32[2,1024,512]{1,2,0:T(8,128)S(1)} collective-permute-done((f32[2,1024,512]{1,2,0:T(8,128)S(1)}, f32[2,1024,512]{1,2,0:T(8,128)S(1)}, u32[]{:S(2)}, u32[]{:S(2)}) %collective-permute-start.2) | collective-permute-done | bytes 4194336 | tf_op jit(solution)/shard_map/ppermute | solution.py:14
  531.1 2.9 add.15
  534.0 0.0 all-gather.5.cloned.1.call-start
  534.0 1.0 copy-done.2
  535.0 0.2 copy.13
  535.2 42.3 %reduce-scatter.5.cloned.1.call-done = f32[2,256,512]{1,2,0:T(8,128)} async-done(((f32[2,1024,512]{1,2,0:T(8,128)}), f32[2,256,512]{1,2,0:T(8,128)}) %reduce-scatter.5.cloned.1.call-update) | async-done | bytes 1048592 | tf_op jit(solution)/shard_map/reduce_scatter | solution.py:57
  577.5 2.1 subtract_convert_fusion
  579.7 0.9 copy.14
  580.5 22.1 %all-gather.5.cloned.1.call-done = bf16[2,1024,512]{1,2,0:T(8,128)(2,1)} async-done(((bf16[2,256,512]{1,2,0:T(8,128)(2,1)}), bf16[2,1024,512]{1,2,0:T(8,128)(2,1)}) %all-gather.5.cloned.1.call-update) | async-done | bytes 2097168 | tf_op jit(solution)/shard_map/all_gather | solution.py:60
  602.6 2.6 fusion.10
  605.2 1.0 copy.15
  (14 shorter events, 0.1 us)
Async XLA Ops:
  7.2 1.6 copy-start
  7.2 100.6 %reduce-scatter.3.cloned.1.call-start = ((), (), s32[]{:S(2)}) async-start(), calls=%async_computation.2 | async-start | bytes 4718592 | tf_op jit(solution)/shard_map/reduce_scatter | solution.py:48
  8.8 3.6 copy-start.4
  11.4 1.0 copy-start.5
  16.2 0.9 copy-start.3
  16.3 144.2 %all-gather.3.cloned.1.call-start = ((), (), s32[]{:S(2)}) async-start(), calls=%async_computation.3 | async-start | bytes 2359296 | tf_op jit(solution)/shard_map/all_gather | solution.py:51
  17.4 145.5 %copy-start.1 = (bf16[2,1024,128]{2,1,0:T(8,128)(2,1)S(1)}, bf16[2,1024,128]{2,1,0:T(8,128)(2,1)}, u32[]{:S(2)}) copy-start(bf16[2,1024,128]{2,1,0:T(8,128)(2,1)} %param.14) | copy-start | bytes 1572868
  109.6 467.9 %reduce-scatter.5.cloned.1.call-start = ((), (), s32[]{:S(2)}) async-start(), calls=%async_computation.4 | async-start | bytes 5242880 | tf_op jit(solution)/shard_map/reduce_scatter | solution.py:57
  163.5 92.2 %collective-permute-start = (f32[2,1024,512]{1,2,0:T(8,128)S(1)}, f32[2,1024,512]{1,2,0:T(8,128)S(1)}, u32[]{:S(2)}, u32[]{:S(2)}) collective-permute-start(f32[2,1024,512]{1,2,0:T(8,128)S(1)} %convolution_bitcast_fusion), channel_id=1, source_target_pairs={{0,4},{4,0},{8,12},{12,8},{16,20},{20,16},{24,28},{28,24},{1,5},{5... | collective-permute-start | bytes 12582920 | tf_op jit(solution)/shard_map/ppermute | solution.py:14
  257.1 91.3 %collective-permute-start.1 = (f32[2,1024,512]{1,2,0:T(8,128)S(1)}, f32[2,1024,512]{1,2,0:T(8,128)S(1)}, u32[]{:S(2)}, u32[]{:S(2)}) collective-permute-start(f32[2,1024,512]{1,2,0:T(8,128)S(1)} %add.13), channel_id=1, source_target_pairs={{0,8},{4,12},{8,0},{12,4},{16,24},{20,28},{24,16},{28,20},{1,9},{5... | collective-permute-start | bytes 12582920 | tf_op jit(solution)/shard_map/ppermute | solution.py:14
  349.8 181.3 %collective-permute-start.2 = (f32[2,1024,512]{1,2,0:T(8,128)S(1)}, f32[2,1024,512]{1,2,0:T(8,128)S(1)}, u32[]{:S(2)}, u32[]{:S(2)}) collective-permute-start(f32[2,1024,512]{1,2,0:T(8,128)S(1)} %add.14), channel_id=1, source_target_pairs={{0,16},{4,20},{8,24},{12,28},{16,0},{20,4},{24,8},{28,12},{1,17},{... | collective-permute-start | bytes 12582920 | tf_op jit(solution)/shard_map/ppermute | solution.py:14
  534.0 1.0 copy-start.2
  534.0 68.7 %all-gather.5.cloned.1.call-start = ((), (), s32[]{:S(2)}) async-start(), calls=%async_computation.5 | async-start | bytes 2621440 | tf_op jit(solution)/shard_map/all_gather | solution.py:60
Sparse Core Ops, SparseCore 0:
  16.4 91.3 reduce-scatter.2
  110.4 49.9 all-gather.2
  534.1 43.3 reduce-scatter.4
  579.8 22.8 all-gather.4
